TPU v7x, 256 devices: a whole 4x4x8 slice. The times are simulated.
256 devices in a mesh: ctx: 32 (over x_lo, z, core), head: 8 (over x_hi, y).
Axes of the slice: x: 4 (x_hi: 2, x_lo: 2; x = x_hi * 2 + x_lo), y: 4, z: 8, core: 2. Of those that a mesh axis runs over, the one named last changes fastest.
Arguments:
- queries: bfloat16 [16384, 16, 128], P('ctx', 'head'), may hold values from -40 to 40
- keys: bfloat16 [16384, 128], P('ctx'), may hold values from -5 to 5
- values: bfloat16 [16384, 128], P('ctx'), may hold values from -1.5 to 1.5
- grad_out: bfloat16 [16384, 16, 128], P('ctx', 'head'), may hold values from -6 to 6
- lengths: int32 [16], replicated, may hold values from 1 to 2048, 16384 in all
- tile_of: int32 [32], replicated, may hold values from 0 to 31, each once
Outputs:
- attended: bfloat16 [16384, 16, 128], P('ctx', 'head')
- grad_queries: bfloat16 [16384, 16, 128], P('ctx', 'head')
- grad_keys: float32 [16384, 128], P('ctx')
- grad_values: float32 [16384, 128], P('ctx')
Inputs may be any that keep to these rules, and one draw needn't show every extreme that they name: 16 positive lengths summing to 16384; the longest is exactly 2048. `tile_of`: each tile number appears once.
All inputs are finite; a program needn't handle non-finite values.
Results may differ from a plain program's by a relative error of at most 0.025.
Values may be sent and summed in bfloat16 or wider, within the bound.
A program may use at most 128 MiB of HBM per device.

v0:
```python
import math

import jax
import jax.numpy as jnp
from jax import lax
from jax.sharding import PartitionSpec as P

NEG_FILL = -1e30


def contract_last(left, right):
    return lax.dot_general(
        left, right, (((1,), (1,)), ((), ())), preferred_element_type=jnp.float32
    )


def contract_first(left, right):
    return lax.dot_general(
        left, right, (((0,), (0,)), ((), ())), preferred_element_type=jnp.float32
    )


def live_test(query_pos, query_doc, key_pos, key_doc):
    return (query_doc[:, None] == key_doc[None, :]) & (key_pos[None, :] <= query_pos[:, None])


def block_probs(
    query_rows, query_pos, query_doc, key_rows, block_pos, block_doc, log_total, score_scale
):
    live_mask = live_test(query_pos, query_doc, block_pos, block_doc)
    scores = contract_last(query_rows, key_rows) * score_scale
    return jnp.where(live_mask, jnp.exp(scores - log_total[:, None]), 0.0)


def on_device(queries, keys, values, grad_out, lengths, tile_of):
    tile_rows, local_heads, head_width = queries.shape
    score_scale = float(head_width) ** (-0.5)
    ctx_count = lax.axis_size("ctx")
    ctx_index = lax.axis_index("ctx")
    offsets = jnp.arange(tile_rows, dtype=jnp.int32)
    key_pos = (tile_of[:, None] * tile_rows + offsets[None, :]).reshape(-1)
    doc_ends = jnp.cumsum(lengths)
    key_doc = jnp.sum((key_pos[:, None] >= doc_ends[None, :]).astype(jnp.int32), axis=1)
    is_mine = jnp.arange(ctx_count, dtype=jnp.int32) == ctx_index
    my_tile = jnp.sum(jnp.where(is_mine, tile_of, 0))
    tile_pos = my_tile * tile_rows + offsets
    tile_doc = jnp.sum((tile_pos[:, None] >= doc_ends[None, :]).astype(jnp.int32), axis=1)
    row_total = tile_rows * local_heads
    query_pos = jnp.repeat(tile_pos, local_heads, total_repeat_length=row_total)
    query_doc = jnp.repeat(tile_doc, local_heads, total_repeat_length=row_total)
    query_rows = queries.reshape(row_total, head_width)
    cotangent_rows = grad_out.reshape(row_total, head_width)
    all_keys, all_values = (
        lax.all_gather(keys, "ctx", axis=0, tiled=True),
        lax.all_gather(values, "ctx", axis=0, tiled=True),
    )
    key_total = all_keys.shape[0]
    key_block = key_total // 16

    def block_slices(begin_row, size_rows):
        return (
            lax.dynamic_slice_in_dim(all_keys, begin_row, size_rows, 0),
            lax.dynamic_slice_in_dim(all_values, begin_row, size_rows, 0),
            lax.dynamic_slice_in_dim(key_pos, begin_row, size_rows, 0),
            lax.dynamic_slice_in_dim(key_doc, begin_row, size_rows, 0),
        )

    def totals_step(loop_index, carried):
        key_rows, value_rows, block_pos, block_doc = block_slices(loop_index * key_block, key_block)
        live_mask = live_test(query_pos, query_doc, block_pos, block_doc)

        def totals_update(state):
            running_max, running_sum = state
            scores = jnp.where(
                live_mask, contract_last(query_rows, key_rows) * score_scale, NEG_FILL
            )
            new_max = jnp.maximum(running_max, jnp.max(scores, axis=1))
            weights = jnp.where(live_mask, jnp.exp(scores - new_max[:, None]), 0.0)
            return (
                new_max,
                running_sum * jnp.exp(running_max - new_max) + jnp.sum(weights, axis=1),
            )

        return lax.cond(jnp.any(live_mask), totals_update, lambda unchanged: unchanged, carried)

    start_state = (
        jnp.full((row_total,), NEG_FILL, jnp.float32),
        jnp.zeros((row_total,), jnp.float32),
    )
    running_max, running_sum = lax.fori_loop(0, 16, totals_step, start_state)
    log_total = running_max + jnp.log(running_sum)

    def attend_step(loop_index, accum):
        key_rows, value_rows, block_pos, block_doc = block_slices(loop_index * key_block, key_block)

        def attend_update(total):
            probs = block_probs(
                query_rows,
                query_pos,
                query_doc,
                key_rows,
                block_pos,
                block_doc,
                log_total,
                score_scale,
            )
            return total + jnp.dot(
                probs.astype(jnp.bfloat16), value_rows, preferred_element_type=jnp.float32
            )

        alive = jnp.any(live_test(query_pos, query_doc, block_pos, block_doc))
        return lax.cond(alive, attend_update, lambda unchanged: unchanged, accum)

    attended = lax.fori_loop(
        0, 16, attend_step, jnp.zeros((row_total, head_width), jnp.float32)
    ).astype(jnp.bfloat16)
    row_delta = jnp.sum(cotangent_rows.astype(jnp.float32) * attended.astype(jnp.float32), axis=1)

    def block_grads(key_rows, value_rows, block_pos, block_doc):
        probs = block_probs(
            query_rows, query_pos, query_doc, key_rows, block_pos, block_doc, log_total, score_scale
        )
        dprob = contract_last(cotangent_rows, value_rows)
        dscore = (probs * (dprob - row_delta[:, None]) * score_scale).astype(jnp.bfloat16)
        return (probs.astype(jnp.bfloat16), dscore)

    def query_step(loop_index, accum):
        key_rows, value_rows, block_pos, block_doc = block_slices(loop_index * key_block, key_block)

        def query_update(total):
            probs_low, dscore = block_grads(key_rows, value_rows, block_pos, block_doc)
            return total + jnp.dot(dscore, key_rows, preferred_element_type=jnp.float32)

        alive = jnp.any(live_test(query_pos, query_doc, block_pos, block_doc))
        return lax.cond(alive, query_update, lambda unchanged: unchanged, accum)

    query_grad = lax.fori_loop(0, 16, query_step, jnp.zeros((row_total, head_width), jnp.float32))
    row_count = lax.axis_size("ctx") * tile_rows
    sub_rows = math.gcd(row_count, key_block)

    def one_block(block_index):
        key_rows, value_rows, block_pos, block_doc = block_slices(block_index * sub_rows, sub_rows)

        def compute(ignored_arg):
            probs_low, dscore = block_grads(key_rows, value_rows, block_pos, block_doc)
            key_part = contract_first(dscore, query_rows)
            value_part = contract_first(probs_low, cotangent_rows)
            return jnp.concatenate([key_part, value_part], axis=1)

        def nothing(ignored_arg):
            return jnp.zeros((sub_rows, 2 * head_width), jnp.float32)

        alive = jnp.any(live_test(query_pos, query_doc, block_pos, block_doc))
        return lax.cond(alive, compute, nothing, 0)

    pieces = lax.map(one_block, jnp.arange(row_count // sub_rows, dtype=jnp.int32))
    partial_rows = lax.psum_scatter(
        pieces.reshape(row_count, 2 * head_width), "ctx", scatter_dimension=0, tiled=True
    )
    grads = lax.psum(partial_rows, "head")
    attended_out = attended.reshape(tile_rows, local_heads, head_width)
    query_out = query_grad.astype(jnp.bfloat16).reshape(tile_rows, local_heads, head_width)
    return (attended_out, query_out, grads[:, :head_width], grads[:, head_width:])


def solution(mesh):
    return jax.shard_map(
        on_device,
        mesh=mesh,
        in_specs=(
            P("ctx", "head", None),
            P("ctx", None),
            P("ctx", None),
            P("ctx", "head", None),
            P(),
            P(),
        ),
        out_specs=(P("ctx", "head", None), P("ctx", "head", None), P("ctx", None), P("ctx", None)),
        check_vma=False,
    )
```

profile of v0, /device:TPU:1, one launch (start us, length us, event | category | flops | bytes accessed | tf_op | source)
XLA Modules:
  0.0 586.9 jit_solution(11838076939264853044)
XLA Ops:
  12.4 6.9 %gather_fusion.1 = s32[1024]{0:T(1024)S(1)} fusion(s32[512]{0:T(512)S(1)} %iota_add_fusion, s32[1024]{0:T(1024)S(1)} %broadcast_clamp_fusion), kind=kCustom, calls=%fused_computation.1.clone | custom fusion | bytes 12288 | tf_op jit(solution)/shard_map/jit(_take)/gather | solution.py:49
  19.3 6.9 %gather_fusion = s32[1024]{0:T(1024)S(1)} fusion(s32[512]{0:T(512)S(1)} %convert_reduce_fusion.1, s32[1024]{0:T(1024)S(1)} %broadcast_clamp_fusion), kind=kCustom, calls=%fused_computation.clone | custom fusion | bytes 12288 | tf_op jit(solution)/shard_map/jit(_take)/gather | solution.py:50
  26.5 53.9 %all-gather.3.cloned.1.call-done = bf16[16384,128]{1,0:T(8,128)(2,1)} async-done(((bf16[512,128]{1,0:T(8,128)(2,1)}), bf16[16384,128]{1,0:T(8,128)(2,1)}) %all-gather.3.cloned.1.call-update) | async-done | bytes 4194320 | tf_op jit(solution)/shard_map/all_gather | solution.py:54
  80.4 54.8 %while.59 = (s32[]{:T(128)}, f32[1024]{0:T(1024)S(1)}, f32[1024]{0:T(1024)S(1)}, s32[1024]{0:T(1024)S(1)}, s32[16384]{0:T(1024)S(1)}, /*index=5*/s32[16384]{0:T(...) while((s32[]{:T(128)}, f32[1024]{0:T(1024)S(1)}, ...), condition=%wide.region_10.12_spmd, body=%wide.region_4.11_spmd.sunk | while | flops 281020416 | bytes 12145425 | solution.py:90
  83.0 3.1 conditional.8
  94.1 3.1 conditional.8
  110.4 3.1 conditional.8
  116.2 3.1 conditional.8
  135.2 13.6 %all-gather.5.cloned.1.call-done = bf16[16384,128]{1,0:T(8,128)(2,1)} async-done(((bf16[512,128]{1,0:T(8,128)(2,1)}), bf16[16384,128]{1,0:T(8,128)(2,1)}) %all-gather.5.cloned.1.call-update) | async-done | bytes 4194320 | tf_op jit(solution)/shard_map/all_gather | solution.py:55
  148.8 55.3 %while.60 = (s32[]{:T(128)}, f32[1024,128]{1,0:T(8,128)S(1)}, s32[1024]{0:T(1024)S(1)}, s32[16384]{0:T(1024)S(1)}, s32[16384]{0:T(1024)S(1)}, /*index=5*/s32[102...) while((s32[]{:T(128)}, f32[1024,128]{1,0:T(8,128)S(1)}, ...), condition=%wide.region_15.17_spmd, body=%wide.region_11.16_spmd.sunk | while | flops 548536320 | bytes 1889561 | solution.py:114
  151.5 2.9 conditional.9
  151.5 2.9 fusion.6
  162.6 2.9 conditional.9
  179.2 2.9 conditional.9
  179.2 2.9 fusion.6
  184.8 2.9 conditional.9
  205.0 133.7 %while.62 = (s32[]{:T(128)}, f32[16,1024,256]{2,1,0:T(8,128)}, s32[1024]{0:T(1024)S(1)}, s32[16]{0:T(128)S(1)}, s32[16384]{0:T(1024)S(1)}, /*index=5*/s32[16384]...) while((s32[]{:T(128)}, f32[16,1024,256]{2,1,0:T(8,128)}, ...), condition=%wide.region_26.28_spmd, body=%wide.region_22.27_spmd.sunk | while | flops 1096024064 | bytes 21575492 | solution.py:156
  208.9 11.6 %conditional.11 = (f32[1,1024,256]{1,2,0:T(8,128)S(1)}) conditional(s32[]{:T(128)} %convert_element_type.95, () %tuple.165, (s32[1024]{0:T(1024)S(1)}, s32[1024]{0:T(1024)S(1)}, s32[1024]{0:T(1024)S(1)}, s32[1024]{0:T(1024)S(1)}, bf16[16384,128]{1,0:T(8,128)(2,1)}, /*index=5*/s32[]{:T(128)}, bf16[1024,128]{1,0:T(8,128)(2,1)S(1)}, ...), branch_computations={%region_24.25_spmd, %region_25.26_spmd} | conditional | flops 1091829760 | bytes 17347592 | solution.py:154
  208.9 3.6 fusion.36
  212.6 4.5 fusion.33
  217.1 3.4 fusion.31
  236.9 11.6 %conditional.11 = (f32[1,1024,256]{1,2,0:T(8,128)S(1)}) conditional(s32[]{:T(128)} %convert_element_type.95, () %tuple.165, (s32[1024]{0:T(1024)S(1)}, s32[1024]{0:T(1024)S(1)}, s32[1024]{0:T(1024)S(1)}, s32[1024]{0:T(1024)S(1)}, bf16[16384,128]{1,0:T(8,128)(2,1)}, /*index=5*/s32[]{:T(128)}, bf16[1024,128]{1,0:T(8,128)(2,1)S(1)}, ...), branch_computations={%region_24.25_spmd, %region_25.26_spmd} | conditional | flops 1091829760 | bytes 17347592 | solution.py:154
  236.9 3.6 fusion.36
  240.5 4.5 fusion.33
  245.0 3.4 fusion.31
  275.7 11.6 %conditional.11 = (f32[1,1024,256]{1,2,0:T(8,128)S(1)}) conditional(s32[]{:T(128)} %convert_element_type.95, () %tuple.165, (s32[1024]{0:T(1024)S(1)}, s32[1024]{0:T(1024)S(1)}, s32[1024]{0:T(1024)S(1)}, s32[1024]{0:T(1024)S(1)}, bf16[16384,128]{1,0:T(8,128)(2,1)}, /*index=5*/s32[]{:T(128)}, bf16[1024,128]{1,0:T(8,128)(2,1)S(1)}, ...), branch_computations={%region_24.25_spmd, %region_25.26_spmd} | conditional | flops 1091829760 | bytes 17347592 | solution.py:154
  275.8 3.6 fusion.36
  279.4 4.5 fusion.33
  283.9 3.4 fusion.31
  292.8 11.6 %conditional.11 = (f32[1,1024,256]{1,2,0:T(8,128)S(1)}) conditional(s32[]{:T(128)} %convert_element_type.95, () %tuple.165, (s32[1024]{0:T(1024)S(1)}, s32[1024]{0:T(1024)S(1)}, s32[1024]{0:T(1024)S(1)}, s32[1024]{0:T(1024)S(1)}, bf16[16384,128]{1,0:T(8,128)(2,1)}, /*index=5*/s32[]{:T(128)}, bf16[1024,128]{1,0:T(8,128)(2,1)S(1)}, ...), branch_computations={%region_24.25_spmd, %region_25.26_spmd} | conditional | flops 1091829760 | bytes 17347592 | solution.py:154
  292.8 3.6 fusion.36
  296.5 4.5 fusion.33
  301.0 3.4 fusion.31
  338.9 152.4 %reduce-scatter.2.cloned.1.call-done = f32[512,256]{1,0:T(8,128)} async-done(((f32[16384,256]{1,0:T(8,128)}), f32[512,256]{1,0:T(8,128)}) %reduce-scatter.2.cloned.1.call-update) | async-done | bytes 524304 | tf_op jit(solution)/shard_map/reduce_scatter | solution.py:157
  491.3 76.4 %while.61 = (s32[]{:T(128)}, f32[1024,128]{1,0:T(8,128)S(1)}, s32[1024]{0:T(1024)S(1)}, s32[16384]{0:T(1024)S(1)}, s32[16384]{0:T(1024)S(1)}, /*index=5*/s32[102...) while((s32[]{:T(128)}, f32[1024,128]{1,0:T(8,128)S(1)}, ...), condition=%wide.region_21.23_spmd, body=%wide.region_17.22_spmd.sunk | while | flops 820117504 | bytes 10807097 | solution.py:137
  494.1 8.2 %conditional.10 = (f32[1024,128]{1,0:T(8,128)S(1)}) conditional(s32[]{:T(128)} %convert_element_type.94, f32[1024,128]{1,0:T(8,128)S(1)} %get-tuple-element.1416, (s32[1024]{0:T(1024)S(1)}, s32[1024]{0:T(1024)S(1)}, s32[1024]{0:T(1024)S(1)}, s32[1024]{0:T(1024)S(1)}, bf16[16384,128]{1,0:T(8,128)(2,1)}, /*index=5*/s32[]{:T(128)}, ...), branch_computations={%region_19.20_spmd, %region_20.21_spmd} | conditional | flops 815923200 | bytes 10774024 | solution.py:135
  494.1 3.6 fusion.21
  497.7 4.6 fusion.17
  510.4 8.2 %conditional.10 = (f32[1024,128]{1,0:T(8,128)S(1)}) conditional(s32[]{:T(128)} %convert_element_type.94, f32[1024,128]{1,0:T(8,128)S(1)} %get-tuple-element.1416, (s32[1024]{0:T(1024)S(1)}, s32[1024]{0:T(1024)S(1)}, s32[1024]{0:T(1024)S(1)}, s32[1024]{0:T(1024)S(1)}, bf16[16384,128]{1,0:T(8,128)(2,1)}, /*index=5*/s32[]{:T(128)}, ...), branch_computations={%region_19.20_spmd, %region_20.21_spmd} | conditional | flops 815923200 | bytes 10774024 | solution.py:135
  510.4 3.6 fusion.21
  514.0 4.6 fusion.17
  532.2 8.2 %conditional.10 = (f32[1024,128]{1,0:T(8,128)S(1)}) conditional(s32[]{:T(128)} %convert_element_type.94, f32[1024,128]{1,0:T(8,128)S(1)} %get-tuple-element.1416, (s32[1024]{0:T(1024)S(1)}, s32[1024]{0:T(1024)S(1)}, s32[1024]{0:T(1024)S(1)}, s32[1024]{0:T(1024)S(1)}, bf16[16384,128]{1,0:T(8,128)(2,1)}, /*index=5*/s32[]{:T(128)}, ...), branch_computations={%region_19.20_spmd, %region_20.21_spmd} | conditional | flops 815923200 | bytes 10774024 | solution.py:135
  532.2 3.6 fusion.21
  535.8 4.6 fusion.17
  543.1 8.2 %conditional.10 = (f32[1024,128]{1,0:T(8,128)S(1)}) conditional(s32[]{:T(128)} %convert_element_type.94, f32[1024,128]{1,0:T(8,128)S(1)} %get-tuple-element.1416, (s32[1024]{0:T(1024)S(1)}, s32[1024]{0:T(1024)S(1)}, s32[1024]{0:T(1024)S(1)}, s32[1024]{0:T(1024)S(1)}, bf16[16384,128]{1,0:T(8,128)(2,1)}, /*index=5*/s32[]{:T(128)}, ...), branch_computations={%region_19.20_spmd, %region_20.21_spmd} | conditional | flops 815923200 | bytes 10774024 | solution.py:135
  543.1 3.6 fusion.21
  546.7 4.6 fusion.17
  568.5 10.1 %all-reduce.2.cloned.1.call-done = f32[512,256]{1,0:T(8,128)} async-done(((f32[512,256]{1,0:T(8,128)}), f32[512,256]{1,0:T(8,128)}) %all-reduce.2.cloned.1.call-update) | async-done | bytes 524304 | tf_op jit(solution)/shard_map/psum | solution.py:160
  (358 shorter events, 190.3 us)
Async XLA Ops:
  7.2 73.2 %all-gather.3.cloned.1.call-start = ((), (), s32[]{:S(2)}) async-start(), calls=%async_computation.1 | async-start | bytes 4325376 | tf_op jit(solution)/shard_map/all_gather | solution.py:54
  7.9 140.8 %all-gather.5.cloned.1.call-start = ((), (), s32[]{:S(2)}) async-start(), calls=%async_computation.2 | async-start | bytes 4325376 | tf_op jit(solution)/shard_map/all_gather | solution.py:55
  8.6 482.6 %reduce-scatter.2.cloned.1.call-start = ((), (), s32[]{:S(2)}) async-start(), calls=%async_computation.3 | async-start | bytes 17301504 | tf_op jit(solution)/shard_map/reduce_scatter | solution.py:157
  12.4 68.1 %copy-start = (bf16[512,2,128]{2,1,0:T(2,128)(2,1)S(1)}, bf16[512,2,128]{2,1,0:T(2,128)(2,1)}, u32[]{:S(2)}) copy-start(bf16[512,2,128]{2,1,0:T(2,128)(2,1)} %param.28) | copy-start | bytes 786436
  148.8 55.4 %copy-start.1 = (bf16[512,2,128]{2,1,0:T(2,128)(2,1)S(1)}, bf16[512,2,128]{2,1,0:T(2,128)(2,1)}, u32[]{:S(2)}) copy-start(bf16[512,2,128]{2,1,0:T(2,128)(2,1)} %param.31) | copy-start | bytes 786436
  338.7 239.8 %all-reduce.2.cloned.1.call-start = ((), (), s32[]{:S(2)}) async-start(), calls=%async_computation.4 | async-start | bytes 1048576 | tf_op jit(solution)/shard_map/psum | solution.py:160
Sparse Core Ops, SparseCore 0:
  9.8 70.5 all-gather.2
  82.3 66.4 all-gather.4
  338.8 152.4 reduce-scatter.1
  493.8 84.7 all-reduce.1
where the time goes:
time: 593 us; the launch traced here: 587 us
  waiting for transfers between devices  231 us (39%)
  other arithmetic  137 us (23%)
  matrix products  97.5 us (16%)
  loops' own time  56 us (9%)
  local copies, waits for them, and re-layouts  50.7 us (9%)
  between operations  14.5 us (2%)
    reduce_scatter x1, waiting for transfers between devices, on_device(): lax.psum_scatter(pieces.reshape(row_count, 2 * head_width), 'ctx', scatte...  152 us
    all_gather x1, waiting for transfers between devices, on_device(): lax.all_gather(keys, 'ctx', axis=0, tiled=True)  53.9 us
    dot_general x12, matrix products, contract_last(): lax.dot_general(left, right, (((1,), (1,)), ((), ())), preferred_element_...  36.2 us
    reduce_or x16, other arithmetic, query_step(): alive = jnp.any(live_test(query_pos, query_doc, block_pos, block_doc))  32.1 us
    reduce_or x16, other arithmetic, attend_step(): alive = jnp.any(live_test(query_pos, query_doc, block_pos, block_doc))  32.1 us
    reduce_or x16, other arithmetic, one_block(): alive = jnp.any(live_test(query_pos, query_doc, block_pos, block_doc))  32.1 us
    dot_general x8, matrix products, contract_first(): lax.dot_general(left, right, (((0,), (0,)), ((), ())), preferred_element_...  31.5 us
    reduce_or x16, other arithmetic, totals_step(): jnp.any(live_mask)  30.7 us
  transfers between devices with their start and end apart: 4, of which 4 were waited for; matrix products, arithmetic and copies ran while one was open for 21% of the time, Pallas kernels for 0%

commit v1 on v0

v1 whole, which is shorter than its diff:
```python
import functools
import math

import jax
import jax.numpy as jnp
from jax import lax
from jax.experimental import pallas as pl
from jax.experimental.pallas import tpu as pltpu
from jax.sharding import PartitionSpec as P

NEG_FILL = -1e30
MESH = pl.DeviceIdType.MESH
BACK = 4
KEY_BLOCK = 256
ROW_CHUNK = 256


def dot(left, right, dims):
    return lax.dot_general(left, right, (dims, ((), ())), preferred_element_type=jnp.float32)


def ctx_of(quad, z, nz):
    return (lax.div(quad, 2) * nz + z) * 2 + lax.rem(quad, 2)


def place(nz, heads):
    ctx = lax.axis_index("ctx")
    head = lax.axis_index("head")
    core = lax.rem(ctx, 2)
    z = lax.rem(lax.div(ctx, 2), nz)
    x_lo = lax.div(ctx, 2 * nz)
    quad = x_lo * 2 + core
    return quad, z, head, quad * heads + head


def greet(quad, z, head, slot, nz, heads):
    barrier = pltpu.get_barrier_semaphore()
    slots = 4 * heads

    @pl.loop(1, slots)
    def _(step):
        other = lax.rem(slot + step, slots)
        target = (ctx_of(lax.div(other, heads), z, nz), lax.rem(other, heads))
        pl.semaphore_signal(barrier, inc=1, device_id=target, device_id_type=MESH)

    @pl.loop(1, nz)
    def _(step):
        target = (ctx_of(quad, lax.rem(z + step, nz), nz), head)
        pl.semaphore_signal(barrier, inc=1, device_id=target, device_id_type=MESH)

    pl.semaphore_wait(barrier, slots - 1 + nz - 1)


def gather_kernel(
    nz,
    heads,
    tiles_ref,
    key_ref,
    value_ref,
    win_ref,
    own,
    zbuf,
    sbuf,
    load_sem,
    qs,
    qr,
    zs,
    zr,
    ps,
    pr,
):
    quad, z, head, slot = place(nz, heads)
    slots = 4 * heads
    part = own.shape[1]
    width = key_ref.shape[-1]
    loads = (
        pltpu.make_async_copy(key_ref, own.at[:, :, 0:width], load_sem.at[0]),
        pltpu.make_async_copy(value_ref, own.at[:, :, width : 2 * width], load_sem.at[1]),
    )
    for copy in loads:
        copy.start()
    greet(quad, z, head, slot, nz, heads)
    for copy in loads:
        copy.wait()

    def quad_copy(step):
        other = lax.rem(quad + step, 4)
        return pltpu.make_async_remote_copy(
            src_ref=own.at[other * heads + head],
            dst_ref=zbuf.at[z, quad],
            send_sem=qs.at[step],
            recv_sem=qr.at[step],
            device_id=(ctx_of(other, z, nz), head),
            device_id_type=MESH,
        )

    for step in range(1, 4):
        quad_copy(step).start()
    mine = pltpu.make_async_copy(own.at[slot], zbuf.at[z, quad], load_sem.at[0])
    whole = pltpu.make_async_copy(own, win_ref.at[BACK], load_sem.at[1])
    mine.start()
    whole.start()
    mine.wait()
    for step in range(1, 4):
        quad_copy(step).wait()

    def z_copy(step):
        return pltpu.make_async_remote_copy(
            src_ref=zbuf.at[z],
            dst_ref=zbuf.at[z],
            send_sem=zs.at[step],
            recv_sem=zr.at[step],
            device_id=(ctx_of(quad, lax.rem(z + step, nz), nz), head),
            device_id_type=MESH,
        )

    @pl.loop(1, nz)
    def _(step):
        z_copy(step).start()

    count = 4 * nz
    wanted = []
    for other in range(4):
        tile = tiles_ref[ctx_of(other, z, nz)]
        for back in range(BACK):
            wanted.append(jnp.maximum(tile - BACK + back, 0))

    def find(index, found):
        tile = tiles_ref[index]
        return tuple(jnp.where(tile == want, index, have) for want, have in zip(wanted, found))

    holders = lax.fori_loop(0, count, find, tuple(jnp.int32(0) for _ in wanted))

    @pl.loop(1, nz)
    def _(step):
        z_copy(step).wait()

    for other in range(4):
        for back in range(BACK):
            holder = holders[other * BACK + back]
            from_z = lax.rem(lax.div(holder, 2), nz)
            from_quad = lax.div(holder, 2 * nz) * 2 + lax.rem(holder, 2)
            sbuf[other, back] = zbuf[from_z, from_quad]

    def plane_copy(step):
        other = lax.rem(slot + step, slots)
        return pltpu.make_async_remote_copy(
            src_ref=sbuf.at[lax.div(other, heads)],
            dst_ref=win_ref.at[0:BACK, slot],
            send_sem=ps.at[step],
            recv_sem=pr.at[step],
            device_id=(ctx_of(lax.div(other, heads), z, nz), lax.rem(other, heads)),
            device_id_type=MESH,
        )

    @pl.loop(1, slots)
    def _(step):
        plane_copy(step).start()

    mine = pltpu.make_async_copy(sbuf.at[quad], win_ref.at[0:BACK, slot], load_sem.at[0])
    mine.start()
    whole.wait()
    mine.wait()

    @pl.loop(1, slots)
    def _(step):
        plane_copy(step).wait()


def gather_window(keys, values, tile_of, nz, heads):
    rows, width = keys.shape
    slots = 4 * heads
    part = rows // slots
    block = (part, 2 * width)
    return pl.pallas_call(
        functools.partial(gather_kernel, nz, heads),
        out_shape=jax.ShapeDtypeStruct((BACK + 1, slots) + block, keys.dtype),
        in_specs=[
            pl.BlockSpec(memory_space=pltpu.SMEM),
            pl.BlockSpec(memory_space=pl.ANY),
            pl.BlockSpec(memory_space=pl.ANY),
        ],
        out_specs=pl.BlockSpec(memory_space=pltpu.VMEM),
        scratch_shapes=[
            pltpu.VMEM((slots,) + block, keys.dtype),
            pltpu.VMEM((nz, 4) + block, keys.dtype),
            pltpu.VMEM((4, BACK) + block, keys.dtype),
            pltpu.SemaphoreType.DMA((2,)),
            pltpu.SemaphoreType.DMA((4,)),
            pltpu.SemaphoreType.DMA((4,)),
            pltpu.SemaphoreType.DMA((nz,)),
            pltpu.SemaphoreType.DMA((nz,)),
            pltpu.SemaphoreType.DMA((slots,)),
            pltpu.SemaphoreType.DMA((slots,)),
        ],
        compiler_params=pltpu.CompilerParams(collective_id=0, has_side_effects=True),
        name="gather_window",
    )(tile_of, keys.reshape(slots, part, width), values.reshape(slots, part, width))


def reduce_kernel(
    nz, heads, tiles_ref, grad_ref, out_ref, rbuf, acc, zsend, zrecv, res, load_sem, gs, gr, zs, zr, fs, fr
):
    quad, z, head, slot = place(nz, heads)
    slots = 4 * heads
    greet(quad, z, head, slot, nz, heads)

    def term_copy(step):
        other = lax.rem(slot + step, slots)
        return pltpu.make_async_remote_copy(
            src_ref=grad_ref.at[:, other],
            dst_ref=rbuf.at[slot],
            send_sem=gs.at[step],
            recv_sem=gr.at[step],
            device_id=(ctx_of(lax.div(other, heads), z, nz), lax.rem(other, heads)),
            device_id_type=MESH,
        )

    @pl.loop(1, slots)
    def _(step):
        term_copy(step).start()

    mine = pltpu.make_async_copy(grad_ref.at[:, slot], rbuf.at[slot], load_sem)
    mine.start()
    mine.wait()

    @pl.loop(1, slots)
    def _(step):
        term_copy(step).wait()

    for other in range(4):
        for back in range(BACK + 1):
            total = rbuf[other * heads, back].astype(jnp.float32)
            for index in range(1, heads):
                total = total + rbuf[other * heads + index, back].astype(jnp.float32)
            acc[other, back] = total

    sources = [tiles_ref[ctx_of(other, z, nz)] - BACK for other in range(4)]

    @pl.loop(0, nz)
    def _(to_z):
        for to_quad in range(4):
            tile = tiles_ref[ctx_of(to_quad, to_z, nz)]
            total = None
            for other in range(4):
                back = tile - sources[other]
                inside = jnp.logical_and(back >= 0, back <= BACK)
                loaded = acc[other, jnp.clip(back, 0, BACK)]
                term = jnp.where(inside, loaded, 0.0)
                total = term if total is None else total + term
            zsend[to_z, to_quad] = total.astype(zsend.dtype)

    def z_copy(step):
        to_z = lax.rem(z + step, nz)
        return pltpu.make_async_remote_copy(
            src_ref=zsend.at[to_z],
            dst_ref=zrecv.at[z],
            send_sem=zs.at[step],
            recv_sem=zr.at[step],
            device_id=(ctx_of(quad, to_z, nz), head),
            device_id_type=MESH,
        )

    @pl.loop(1, nz)
    def _(step):
        z_copy(step).start()

    mine = pltpu.make_async_copy(zsend.at[z], zrecv.at[z], load_sem)
    mine.start()
    mine.wait()

    @pl.loop(1, nz)
    def _(step):
        z_copy(step).wait()

    total = zrecv[0].astype(jnp.float32)
    for index in range(1, nz):
        total = total + zrecv[index].astype(jnp.float32)
    res[...] = total.astype(res.dtype)

    def final_copy(step):
        other = lax.rem(slot + step, slots)
        return pltpu.make_async_remote_copy(
            src_ref=res.at[lax.div(other, heads)],
            dst_ref=out_ref.at[slot],
            send_sem=fs.at[step],
            recv_sem=fr.at[step],
            device_id=(ctx_of(lax.div(other, heads), z, nz), lax.rem(other, heads)),
            device_id_type=MESH,
        )

    @pl.loop(1, slots)
    def _(step):
        final_copy(step).start()

    mine = pltpu.make_async_copy(res.at[quad], out_ref.at[slot], load_sem)
    mine.start()
    mine.wait()

    @pl.loop(1, slots)
    def _(step):
        final_copy(step).wait()


def reduce_terms(terms, tile_of, nz, heads):
    slots = 4 * heads
    block = terms.shape[2:]
    low = terms.dtype
    return pl.pallas_call(
        functools.partial(reduce_kernel, nz, heads),
        out_shape=jax.ShapeDtypeStruct((slots,) + block, low),
        in_specs=[
            pl.BlockSpec(memory_space=pltpu.SMEM),
            pl.BlockSpec(memory_space=pltpu.VMEM),
        ],
        out_specs=pl.BlockSpec(memory_space=pltpu.VMEM),
        scratch_shapes=[
            pltpu.VMEM((slots, BACK + 1) + block, low),
            pltpu.VMEM((4, BACK + 1) + block, jnp.float32),
            pltpu.VMEM((nz, 4) + block, low),
            pltpu.VMEM((nz, 4) + block, low),
            pltpu.VMEM((4,) + block, low),
            pltpu.SemaphoreType.DMA,
            pltpu.SemaphoreType.DMA((slots,)),
            pltpu.SemaphoreType.DMA((slots,)),
            pltpu.SemaphoreType.DMA((nz,)),
            pltpu.SemaphoreType.DMA((nz,)),
            pltpu.SemaphoreType.DMA((slots,)),
            pltpu.SemaphoreType.DMA((slots,)),
        ],
        compiler_params=pltpu.CompilerParams(collective_id=1, has_side_effects=True),
        name="reduce_terms",
    )(tile_of, terms)


def attention_kernel(
    local_heads,
    own_ctx_ref,
    tiles_ref,
    lengths_ref,
    query_ref,
    cot_ref,
    win_ref,
    att_ref,
    dq_ref,
    grad_ref,
    s_scr,
    p_scr,
    dk_acc,
    dv_acc,
):
    row_total, width = query_ref.shape
    keys_total = win_ref.shape[0]
    tile_rows = row_total // local_heads
    scale = float(width) ** -0.5
    log_scale = scale * math.log2(math.e)
    tile = tiles_ref[own_ctx_ref[0]]
    base = (tile - BACK) * tile_rows
    chunk_pos = ROW_CHUNK // local_heads
    dk_acc[...] = jnp.zeros_like(dk_acc)
    dv_acc[...] = jnp.zeros_like(dv_acc)
    doc_ends = []
    running = jnp.int32(0)
    for index in range(lengths_ref.shape[0]):
        running = running + lengths_ref[index]
        doc_ends.append(running)

    for chunk in range(row_total // ROW_CHUNK):
        rows = pl.ds(chunk * ROW_CHUNK, ROW_CHUNK)
        first_pos = tile * tile_rows + chunk * chunk_pos
        pos = first_pos + lax.broadcasted_iota(jnp.int32, (1, ROW_CHUNK), 1) // local_heads
        low = jnp.zeros_like(pos)
        low_first = jnp.int32(0)
        for end in doc_ends:
            low = jnp.where(pos >= end, end, low)
            low_first = jnp.where(first_pos >= end, end, low_first)
        low = low - base
        high = pos - base
        first_block = (low_first - base) // KEY_BLOCK
        last_block = (BACK * tile_rows + (chunk + 1) * chunk_pos + KEY_BLOCK - 1) // KEY_BLOCK
        q = query_ref[rows, :]

        def score_step(block, top):
            begin = pl.multiple_of(block * KEY_BLOCK, KEY_BLOCK)
            k = win_ref[pl.ds(begin, KEY_BLOCK), 0:width]
            s = dot(k, q, ((1,), (1,)))
            at = begin + lax.broadcasted_iota(jnp.int32, s.shape, 0)
            s = jnp.where((at >= low) & (at <= high), s, NEG_FILL)
            s_scr[pl.ds(begin, KEY_BLOCK), :] = s
            return jnp.maximum(top, jnp.max(s.reshape(KEY_BLOCK // 8, 8, ROW_CHUNK), axis=0))

        top = lax.fori_loop(
            first_block, last_block, score_step, jnp.full((8, ROW_CHUNK), NEG_FILL, jnp.float32)
        )
        top = jnp.max(top, axis=0, keepdims=True) * log_scale

        def prob_step(block, carried):
            total, out = carried
            begin = pl.multiple_of(block * KEY_BLOCK, KEY_BLOCK)
            p = jnp.exp2(s_scr[pl.ds(begin, KEY_BLOCK), :] * log_scale - top)
            total = total + jnp.sum(p.reshape(KEY_BLOCK // 8, 8, ROW_CHUNK), axis=0)
            p_low = p.astype(jnp.bfloat16)
            p_scr[pl.ds(begin, KEY_BLOCK), :] = p_low
            v = win_ref[pl.ds(begin, KEY_BLOCK), width : 2 * width]
            return total, out + dot(v, p_low, ((0,), (0,)))

        total, out = lax.fori_loop(
            first_block,
            last_block,
            prob_step,
            (jnp.zeros((8, ROW_CHUNK), jnp.float32), jnp.zeros((width, ROW_CHUNK), jnp.float32)),
        )
        inverse = 1.0 / jnp.sum(total, axis=0, keepdims=True)
        out = (out * inverse).astype(jnp.bfloat16).astype(jnp.float32)
        att_ref[rows, :] = out.T.astype(jnp.bfloat16)
        cot = cot_ref[rows, :].astype(jnp.float32).T
        delta = jnp.sum(cot * out, axis=0, keepdims=True) * inverse
        cot_scaled = cot * inverse
        cot_low = cot_scaled.astype(jnp.bfloat16)
        cot_rows = cot_scaled.T.astype(jnp.bfloat16)

        def grad_step(block, dq):
            begin = pl.multiple_of(block * KEY_BLOCK, KEY_BLOCK)
            keys_at = pl.ds(begin, KEY_BLOCK)
            k = win_ref[keys_at, 0:width]
            v = win_ref[keys_at, width : 2 * width]
            p_low = p_scr[keys_at, :]
            dp = dot(v, cot_low, ((1,), (0,)))
            ds = (p_low.astype(jnp.float32) * (dp - delta)).astype(jnp.bfloat16)
            dv_acc[keys_at, :] += dot(p_low, cot_rows, ((1,), (0,)))
            dk_acc[keys_at, :] += dot(ds, q, ((1,), (0,)))
            return dq + dot(k, ds, ((0,), (0,)))

        dq = lax.fori_loop(
            first_block, last_block, grad_step, jnp.zeros((width, ROW_CHUNK), jnp.float32)
        )
        dq_ref[rows, :] = (dq * scale).T.astype(jnp.bfloat16)

    grad_ref[:, 0:width] = (dk_acc[...] * scale).astype(jnp.bfloat16)
    grad_ref[:, width : 2 * width] = dv_acc[...].astype(jnp.bfloat16)


def attention(own_ctx, tile_of, lengths, query_rows, cot_rows, window, local_heads):
    row_total, width = query_rows.shape
    keys_total = window.shape[0]
    smem = pl.BlockSpec(memory_space=pltpu.SMEM)
    vmem = pl.BlockSpec(memory_space=pltpu.VMEM)
    return pl.pallas_call(
        functools.partial(attention_kernel, local_heads),
        out_shape=(
            jax.ShapeDtypeStruct((row_total, width), jnp.bfloat16),
            jax.ShapeDtypeStruct((row_total, width), jnp.bfloat16),
            jax.ShapeDtypeStruct((keys_total, 2 * width), jnp.bfloat16),
        ),
        in_specs=[smem, smem, smem, vmem, vmem, vmem],
        out_specs=(vmem, vmem, vmem),
        scratch_shapes=[
            pltpu.VMEM((keys_total, ROW_CHUNK), jnp.float32),
            pltpu.VMEM((keys_total, ROW_CHUNK), jnp.bfloat16),
            pltpu.VMEM((keys_total, width), jnp.float32),
            pltpu.VMEM((keys_total, width), jnp.float32),
        ],
        compiler_params=pltpu.CompilerParams(vmem_limit_bytes=40 * 1024 * 1024),
        name="attention",
    )(own_ctx, tile_of, lengths, query_rows, cot_rows, window)


def on_device(ctx_count, heads, queries, keys, values, grad_out, lengths, tile_of):
    tile_rows, local_heads, width = queries.shape
    nz = ctx_count // 4
    slots = 4 * heads
    part = tile_rows // slots
    window = gather_window(keys, values, tile_of, nz, heads)
    own_ctx = lax.axis_index("ctx").astype(jnp.int32).reshape(1)
    attended, query_grad, terms = attention(
        own_ctx,
        tile_of,
        lengths,
        queries.reshape(-1, width),
        grad_out.reshape(-1, width),
        window.reshape((BACK + 1) * tile_rows, 2 * width),
        local_heads,
    )
    sums = reduce_terms(
        terms.reshape(BACK + 1, slots, part, 2 * width), tile_of, nz, heads
    ).reshape(tile_rows, 2 * width)
    return (
        attended.reshape(queries.shape),
        query_grad.reshape(queries.shape),
        sums[:, :width].astype(jnp.float32),
        sums[:, width:].astype(jnp.float32),
    )


def solution(mesh):
    return jax.shard_map(
        functools.partial(on_device, mesh.shape["ctx"], mesh.shape["head"]),
        mesh=mesh,
        in_specs=(
            P("ctx", "head", None),
            P("ctx", None),
            P("ctx", None),
            P("ctx", "head", None),
            P(),
            P(),
        ),
        out_specs=(P("ctx", "head", None), P("ctx", "head", None), P("ctx", None), P("ctx", None)),
        check_vma=False,
    )
```

time: 593 us -> 108 us (0.18); the launches traced: 587 us -> 109 us
  waiting for transfers between devices: 231 us -> 0 us
  other arithmetic: 137 us -> 1.79 us
  Pallas kernels: 0 us -> 104 us
  matrix products: 97.5 us -> 0 us
  loops' own time: 56 us -> 0 us
  local copies, waits for them, and re-layouts: 50.7 us -> 2.4 us
  between operations: 14.5 us -> 0.73 us
    reduce_scatter x1 -> x0, waiting for transfers between devices: 152 us -> none  [on_device(): lax.psum_scatter(pieces.reshape(row_count, 2 * head_width), 'ctx', scatte...]
    reduce_or x64 -> x0, other arithmetic: 127 us -> none  [the longest x16 32.1 us: query_step(): alive = jnp.any(live_test(query_pos, query_doc, block_pos, block_doc))]
    pallas_call x0 -> x3, Pallas kernels: none -> 104 us  [the longest x1 55.4 us: reduce_terms(): pl.pallas_call(functools.partial(reduce_kernel, nz, heads), out_shape=jax...]
    dot_general x28 -> x0, matrix products: 97.5 us -> none  [the longest x12 36.2 us: contract_last(): lax.dot_general(left, right, (((1,), (1,)), ((), ())), preferred_element_...]
    all_gather x2 -> x0, waiting for transfers between devices: 67.5 us -> none  [the longest x1 53.9 us: on_device(): lax.all_gather(keys, 'ctx', axis=0, tiled=True)]
    another operation x68 -> x0, loops' own time: 56 us -> none  [the longest x1 21.5 us: on_device(): lax.map(one_block, jnp.arange(row_count // sub_rows, dtype=jnp.int32))]
    dynamic_update_slice x32 -> x0, local copies, waits for them, and re-layouts: 22.4 us -> none  [on_device(): lax.map(one_block, jnp.arange(row_count // sub_rows, dtype=jnp.int32))]
    gather x2 -> x0, local copies, waits for them, and re-layouts: 13.7 us -> none  [the longest x1 6.86 us: on_device(): query_doc = jnp.repeat(tile_doc, local_heads, total_repeat_length=row_total)]
  transfers between devices with their start and end apart: 4 -> 0, of which waited for: 4 -> 0; matrix products, arithmetic and copies ran while one was open for 21% -> 0% of each run, Pallas kernels for 0% -> 0%
where the time goes in v1:
time: 108 us; the launch traced here: 109 us
  Pallas kernels  104 us (96%)
  local copies, waits for them, and re-layouts  2.4 us (2%)
  other arithmetic  1.79 us (2%)
    pallas_call x1, Pallas kernels, reduce_terms(): pl.pallas_call(functools.partial(reduce_kernel, nz, heads), out_shape=jax...  55.4 us
    pallas_call x1, Pallas kernels, gather_window(): pl.pallas_call(functools.partial(gather_kernel, nz, heads), out_shape=jax...  38.3 us
    pallas_call x1, Pallas kernels, attention(): pl.pallas_call(functools.partial(attention_kernel, local_heads), out_shap...  10.4 us
    unnamed x12, local copies, waits for them, and re-layouts  2.4 us

profile of v1, /device:TPU:1, one launch (start us, length us, event | category | flops | bytes accessed | tf_op | source)
XLA Modules:
  0.0 109.0 jit_solution(15934066943898283999)
XLA Ops:
  0.6 0.0 copy-start.4
  0.6 0.0 copy-start.5
  0.7 0.0 copy-start.3
  0.7 0.0 copy-start.2
  0.7 38.3 %gather_window.1 = bf16[5,32,16,256]{3,2,1,0:T(8,128)(2,1)} custom-call(s32[32]{0:T(128)} %tiles_ref.5, bf16[32,16,128]{2,1,0:T(8,128)(2,1)} %bitcast.15, bf16[32,16,128]{2,1,0:T(8,128)(2,1)} %bitcast.16), custom_call_target="tpu_custom_call" | custom-call | tf_op jit(solution)/shard_map/gather_window/pallas_call | solution.py:175
  39.0 0.0 copy-done.4
  39.0 0.0 copy-done.5
  39.0 0.0 copy-done.3
  39.0 0.0 copy-done.2
  39.0 0.0 copy-start
  39.0 1.3 %copy-done = bf16[5,32,16,256]{3,2,1,0:T(8,128)(2,1)S(1)} copy-done((bf16[5,32,16,256]{3,2,1,0:T(8,128)(2,1)S(1)}, bf16[5,32,16,256]{3,2,1,0:T(8,128)(2,1)}, u32[]{:S(2)}) %copy-start) | copy-done | bytes 1310744
  40.3 10.4 %attention.1 = (bf16[1024,128]{1,0:T(8,128)(2,1)}, bf16[1024,128]{1,0:T(8,128)(2,1)}, bf16[2560,256]{1,0:T(8,128)(2,1)S(1)}) custom-call(s32[1]{0:T(128)} %bitcast.own_ctx_ref, s32[32]{0:T(128)S(1)} %copy-done.4, s32[16]{0:T(128)S(1)} %copy-done.5, bf16[1024,128]{1,0:T(8,128)(2,1)S(1)} %bitcast.12, bf16[1024,128]{1,0:T(8,128)(2,1)S(1)} %bitcast.13, ...), custom_call_target="tpu_custom_call" | custom-call | tf_op jit(solution)/shard_map/attention/pallas_call | solution.py:448
  50.7 0.0 copy-start.1
  50.7 1.1 copy-done.1
  51.8 55.4 %reduce_terms.1 = bf16[32,16,256]{2,1,0:T(8,128)(2,1)} custom-call(s32[32]{0:T(128)} %tiles_ref.5, bf16[5,32,16,256]{3,2,1,0:T(8,128)(2,1)} %bitcast.11), custom_call_target="tpu_custom_call" | custom-call | tf_op jit(solution)/shard_map/reduce_terms/pallas_call | solution.py:309
  107.2 1.8 %slice_convert_fusion = (f32[512,128]{1,0:T(8,128)}, f32[512,128]{1,0:T(8,128)}) fusion(bf16[512,256]{1,0:T(8,128)(2,1)} %bitcast.14), kind=kLoop, calls=%fused_computation | loop fusion | flops 131072 | bytes 786432 | tf_op jit(solution)/shard_map/convert_element_type | solution.py:491
Async XLA Ops:
  0.6 38.3 %copy-start.4 = (s32[32]{0:T(128)S(1)}, s32[32]{0:T(128)}, u32[]{:S(2)}) copy-start(s32[32]{0:T(128)} %tiles_ref.5) | copy-start | bytes 388
  0.6 38.3 %copy-start.5 = (s32[16]{0:T(128)S(1)}, s32[16]{0:T(128)}, u32[]{:S(2)}) copy-start(s32[16]{0:T(128)} %lengths_ref.1) | copy-start | bytes 196
  0.7 38.3 %copy-start.3 = (bf16[512,2,128]{2,1,0:T(2,128)(2,1)S(1)}, bf16[512,2,128]{2,1,0:T(2,128)(2,1)}, u32[]{:S(2)}) copy-start(bf16[512,2,128]{2,1,0:T(2,128)(2,1)} %param.9) | copy-start | bytes 786436
  0.7 38.3 %copy-start.2 = (bf16[512,2,128]{2,1,0:T(2,128)(2,1)S(1)}, bf16[512,2,128]{2,1,0:T(2,128)(2,1)}, u32[]{:S(2)}) copy-start(bf16[512,2,128]{2,1,0:T(2,128)(2,1)} %param.6) | copy-start | bytes 786436
  39.0 1.3 %copy-start = (bf16[5,32,16,256]{3,2,1,0:T(8,128)(2,1)S(1)}, bf16[5,32,16,256]{3,2,1,0:T(8,128)(2,1)}, u32[]{:S(2)}) copy-start(bf16[5,32,16,256]{3,2,1,0:T(8,128)(2,1)} %gather_window.1) | copy-start | bytes 3932164
  50.7 1.1 copy-start.1

commit v2 on v1

--- a/solution.py
+++ b/solution.py
@@ -11,8 +11,8 @@
 NEG_FILL = -1e30
 MESH = pl.DeviceIdType.MESH
 BACK = 4
-KEY_BLOCK = 256
-ROW_CHUNK = 256
+KEY_BLOCK = 512
+ROW_CHUNK = 1024
 
 
 def dot(left, right, dims):
@@ -357,8 +357,6 @@
     tile = tiles_ref[own_ctx_ref[0]]
     base = (tile - BACK) * tile_rows
     chunk_pos = ROW_CHUNK // local_heads
-    dk_acc[...] = jnp.zeros_like(dk_acc)
-    dv_acc[...] = jnp.zeros_like(dv_acc)
     doc_ends = []
     running = jnp.int32(0)
     for index in range(lengths_ref.shape[0]):
@@ -370,46 +368,33 @@
         first_pos = tile * tile_rows + chunk * chunk_pos
         pos = first_pos + lax.broadcasted_iota(jnp.int32, (1, ROW_CHUNK), 1) // local_heads
         low = jnp.zeros_like(pos)
-        low_first = jnp.int32(0)
         for end in doc_ends:
             low = jnp.where(pos >= end, end, low)
-            low_first = jnp.where(first_pos >= end, end, low_first)
         low = low - base
         high = pos - base
-        first_block = (low_first - base) // KEY_BLOCK
-        last_block = (BACK * tile_rows + (chunk + 1) * chunk_pos + KEY_BLOCK - 1) // KEY_BLOCK
         q = query_ref[rows, :]
-
-        def score_step(block, top):
-            begin = pl.multiple_of(block * KEY_BLOCK, KEY_BLOCK)
-            k = win_ref[pl.ds(begin, KEY_BLOCK), 0:width]
-            s = dot(k, q, ((1,), (1,)))
-            at = begin + lax.broadcasted_iota(jnp.int32, s.shape, 0)
-            s = jnp.where((at >= low) & (at <= high), s, NEG_FILL)
-            s_scr[pl.ds(begin, KEY_BLOCK), :] = s
-            return jnp.maximum(top, jnp.max(s.reshape(KEY_BLOCK // 8, 8, ROW_CHUNK), axis=0))
-
-        top = lax.fori_loop(
-            first_block, last_block, score_step, jnp.full((8, ROW_CHUNK), NEG_FILL, jnp.float32)
-        )
+        blocks = range(0, keys_total, KEY_BLOCK)
+        top = jnp.full((8, ROW_CHUNK), NEG_FILL, jnp.float32)
+        at = lax.broadcasted_iota(jnp.int32, (KEY_BLOCK, ROW_CHUNK), 0)
+        for begin in blocks:
+            keys_at = pl.ds(begin, KEY_BLOCK)
+            s = dot(win_ref[keys_at, 0:width], q, ((1,), (1,)))
+            live = at >= low - begin
+            if begin + KEY_BLOCK > BACK * tile_rows:
+                live = live & (at <= high - begin)
+            s = jnp.where(live, s, NEG_FILL)
+            s_scr[keys_at, :] = s
+            top = jnp.maximum(top, jnp.max(s.reshape(KEY_BLOCK // 8, 8, ROW_CHUNK), axis=0))
         top = jnp.max(top, axis=0, keepdims=True) * log_scale
-
-        def prob_step(block, carried):
-            total, out = carried
-            begin = pl.multiple_of(block * KEY_BLOCK, KEY_BLOCK)
-            p = jnp.exp2(s_scr[pl.ds(begin, KEY_BLOCK), :] * log_scale - top)
+        total = jnp.zeros((8, ROW_CHUNK), jnp.float32)
+        out = jnp.zeros((width, ROW_CHUNK), jnp.float32)
+        for begin in blocks:
+            keys_at = pl.ds(begin, KEY_BLOCK)
+            p = jnp.exp2(s_scr[keys_at, :] * log_scale - top)
             total = total + jnp.sum(p.reshape(KEY_BLOCK // 8, 8, ROW_CHUNK), axis=0)
             p_low = p.astype(jnp.bfloat16)
-            p_scr[pl.ds(begin, KEY_BLOCK), :] = p_low
-            v = win_ref[pl.ds(begin, KEY_BLOCK), width : 2 * width]
-            return total, out + dot(v, p_low, ((0,), (0,)))
-
-        total, out = lax.fori_loop(
-            first_block,
-            last_block,
-            prob_step,
-            (jnp.zeros((8, ROW_CHUNK), jnp.float32), jnp.zeros((width, ROW_CHUNK), jnp.float32)),
-        )
+            p_scr[keys_at, :] = p_low
+            out = out + dot(win_ref[keys_at, width : 2 * width], p_low, ((0,), (0,)))
         inverse = 1.0 / jnp.sum(total, axis=0, keepdims=True)
         out = (out * inverse).astype(jnp.bfloat16).astype(jnp.float32)
         att_ref[rows, :] = out.T.astype(jnp.bfloat16)
@@ -418,26 +403,18 @@
         cot_scaled = cot * inverse
         cot_low = cot_scaled.astype(jnp.bfloat16)
         cot_rows = cot_scaled.T.astype(jnp.bfloat16)
-
-        def grad_step(block, dq):
-            begin = pl.multiple_of(block * KEY_BLOCK, KEY_BLOCK)
+        dq = jnp.zeros((width, ROW_CHUNK), jnp.float32)
+        for begin in blocks:
             keys_at = pl.ds(begin, KEY_BLOCK)
             k = win_ref[keys_at, 0:width]
             v = win_ref[keys_at, width : 2 * width]
             p_low = p_scr[keys_at, :]
             dp = dot(v, cot_low, ((1,), (0,)))
             ds = (p_low.astype(jnp.float32) * (dp - delta)).astype(jnp.bfloat16)
-            dv_acc[keys_at, :] += dot(p_low, cot_rows, ((1,), (0,)))
-            dk_acc[keys_at, :] += dot(ds, q, ((1,), (0,)))
-            return dq + dot(k, ds, ((0,), (0,)))
-
-        dq = lax.fori_loop(
-            first_block, last_block, grad_step, jnp.zeros((width, ROW_CHUNK), jnp.float32)
-        )
+            grad_ref[keys_at, width : 2 * width] = dot(p_low, cot_rows, ((1,), (0,))).astype(jnp.bfloat16)
+            grad_ref[keys_at, 0:width] = (dot(ds, q, ((1,), (0,))) * scale).astype(jnp.bfloat16)
+            dq = dq + dot(k, ds, ((0,), (0,)))
         dq_ref[rows, :] = (dq * scale).T.astype(jnp.bfloat16)
-
-    grad_ref[:, 0:width] = (dk_acc[...] * scale).astype(jnp.bfloat16)
-    grad_ref[:, width : 2 * width] = dv_acc[...].astype(jnp.bfloat16)
 
 
 def attention(own_ctx, tile_of, lengths, query_rows, cot_rows, window, local_heads):

time: 108 us -> 95.3 us (0.88); the launches traced: 109 us -> 95.1 us
  Pallas kernels: 104 us -> 90.2 us
    pallas_call x1, Pallas kernels: 55.4 us -> 40.7 us  [reduce_terms(): pl.pallas_call(functools.partial(reduce_kernel, nz, heads), out_shape=jax...]
where the time goes in v2:
time: 95.3 us; the launch traced here: 95.1 us
  Pallas kernels  90.2 us (95%)
  local copies, waits for them, and re-layouts  2.4 us (3%)
  other arithmetic  1.79 us (2%)
    pallas_call x1, Pallas kernels, reduce_terms(): pl.pallas_call(functools.partial(reduce_kernel, nz, heads), out_shape=jax...  40.7 us
    pallas_call x1, Pallas kernels, gather_window(): pl.pallas_call(functools.partial(gather_kernel, nz, heads), out_shape=jax...  38.3 us
    pallas_call x1, Pallas kernels, attention(): pl.pallas_call(functools.partial(attention_kernel, local_heads), out_shap...  11.2 us
    unnamed x12, local copies, waits for them, and re-layouts  2.4 us

profile of v2, /device:TPU:1, one launch (start us, length us, event | category | flops | bytes accessed | tf_op | source)
XLA Modules:
  0.0 95.1 jit_solution(14397085667925913064)
XLA Ops:
  0.6 0.0 copy-start.4
  0.6 0.0 copy-start.5
  0.7 0.0 copy-start.3
  0.7 0.0 copy-start.2
  0.7 38.3 %gather_window.1 = bf16[5,32,16,256]{3,2,1,0:T(8,128)(2,1)} custom-call(s32[32]{0:T(128)} %tiles_ref.5, bf16[32,16,128]{2,1,0:T(8,128)(2,1)} %bitcast.15, bf16[32,16,128]{2,1,0:T(8,128)(2,1)} %bitcast.16), custom_call_target="tpu_custom_call" | custom-call | tf_op jit(solution)/shard_map/gather_window/pallas_call | solution.py:175
  39.0 0.0 copy-done.4
  39.0 0.0 copy-done.5
  39.0 0.0 copy-done.3
  39.0 0.0 copy-done.2
  39.0 0.0 copy-start
  39.0 1.3 %copy-done = bf16[5,32,16,256]{3,2,1,0:T(8,128)(2,1)S(1)} copy-done((bf16[5,32,16,256]{3,2,1,0:T(8,128)(2,1)S(1)}, bf16[5,32,16,256]{3,2,1,0:T(8,128)(2,1)}, u32[]{:S(2)}) %copy-start) | copy-done | bytes 1310744
  40.3 11.2 %attention.1 = (bf16[1024,128]{1,0:T(8,128)(2,1)}, bf16[1024,128]{1,0:T(8,128)(2,1)}, bf16[2560,256]{1,0:T(8,128)(2,1)S(1)}) custom-call(s32[1]{0:T(128)} %bitcast.own_ctx_ref, s32[32]{0:T(128)S(1)} %copy-done.4, s32[16]{0:T(128)S(1)} %copy-done.5, bf16[1024,128]{1,0:T(8,128)(2,1)S(1)} %bitcast.12, bf16[1024,128]{1,0:T(8,128)(2,1)S(1)} %bitcast.13, ...), custom_call_target="tpu_custom_call" | custom-call | tf_op jit(solution)/shard_map/attention/pallas_call | solution.py:425
  51.6 0.0 copy-start.1
  51.6 1.1 %copy-done.1 = bf16[2560,256]{1,0:T(8,128)(2,1)} copy-done((bf16[2560,256]{1,0:T(8,128)(2,1)}, bf16[2560,256]{1,0:T(8,128)(2,1)S(1)}, u32[]{:S(2)}) %copy-start.1) | copy-done | bytes 1310744
  52.6 40.7 %reduce_terms.1 = bf16[32,16,256]{2,1,0:T(8,128)(2,1)} custom-call(s32[32]{0:T(128)} %tiles_ref.5, bf16[5,32,16,256]{3,2,1,0:T(8,128)(2,1)} %bitcast.11), custom_call_target="tpu_custom_call" | custom-call | tf_op jit(solution)/shard_map/reduce_terms/pallas_call | solution.py:309
  93.3 1.8 %slice_convert_fusion = (f32[512,128]{1,0:T(8,128)}, f32[512,128]{1,0:T(8,128)}) fusion(bf16[512,256]{1,0:T(8,128)(2,1)} %bitcast.14), kind=kLoop, calls=%fused_computation | loop fusion | flops 131072 | bytes 786432 | tf_op jit(solution)/shard_map/convert_element_type | solution.py:468
Async XLA Ops:
  0.6 38.3 %copy-start.4 = (s32[32]{0:T(128)S(1)}, s32[32]{0:T(128)}, u32[]{:S(2)}) copy-start(s32[32]{0:T(128)} %tiles_ref.5) | copy-start | bytes 388
  0.6 38.3 %copy-start.5 = (s32[16]{0:T(128)S(1)}, s32[16]{0:T(128)}, u32[]{:S(2)}) copy-start(s32[16]{0:T(128)} %lengths_ref.1) | copy-start | bytes 196
  0.7 38.3 %copy-start.3 = (bf16[512,2,128]{2,1,0:T(2,128)(2,1)S(1)}, bf16[512,2,128]{2,1,0:T(2,128)(2,1)}, u32[]{:S(2)}) copy-start(bf16[512,2,128]{2,1,0:T(2,128)(2,1)} %param.9) | copy-start | bytes 786436
  0.7 38.3 %copy-start.2 = (bf16[512,2,128]{2,1,0:T(2,128)(2,1)S(1)}, bf16[512,2,128]{2,1,0:T(2,128)(2,1)}, u32[]{:S(2)}) copy-start(bf16[512,2,128]{2,1,0:T(2,128)(2,1)} %param.6) | copy-start | bytes 786436
  39.0 1.3 %copy-start = (bf16[5,32,16,256]{3,2,1,0:T(8,128)(2,1)S(1)}, bf16[5,32,16,256]{3,2,1,0:T(8,128)(2,1)}, u32[]{:S(2)}) copy-start(bf16[5,32,16,256]{3,2,1,0:T(8,128)(2,1)} %gather_window.1) | copy-start | bytes 3932164
  51.6 1.1 %copy-start.1 = (bf16[2560,256]{1,0:T(8,128)(2,1)}, bf16[2560,256]{1,0:T(8,128)(2,1)S(1)}, u32[]{:S(2)}) copy-start(bf16[2560,256]{1,0:T(8,128)(2,1)S(1)} %get-tuple-element.9) | copy-start | bytes 3932164

commit v3 on v0

v3 whole, which is shorter than its diff:
```python
import functools
import math

import jax
import jax.numpy as jnp
from jax import lax
from jax.experimental import pallas as pl
from jax.experimental.pallas import tpu as pltpu
from jax.sharding import PartitionSpec as P

NEG_FILL = -1e30
MESH = pl.DeviceIdType.MESH
BACK = 4


def dot(left, right, dims):
    return lax.dot_general(left, right, (dims, ((), ())), preferred_element_type=jnp.float32)


def ctx_of(quad, z, nz):
    return (lax.div(quad, 2) * nz + z) * 2 + lax.rem(quad, 2)


def place(nz, heads):
    ctx = lax.axis_index("ctx")
    head = lax.axis_index("head")
    core = lax.rem(ctx, 2)
    z = lax.rem(lax.div(ctx, 2), nz)
    x_lo = lax.div(ctx, 2 * nz)
    quad = x_lo * 2 + core
    return quad, z, head, quad * heads + head


def greet(quad, z, head, slot, nz, heads):
    barrier = pltpu.get_barrier_semaphore()
    slots = 4 * heads

    @pl.loop(1, slots)
    def _(step):
        other = lax.rem(slot + step, slots)
        target = (ctx_of(lax.div(other, heads), z, nz), lax.rem(other, heads))
        pl.semaphore_signal(barrier, inc=1, device_id=target, device_id_type=MESH)

    @pl.loop(1, nz)
    def _(step):
        target = (ctx_of(quad, lax.rem(z + step, nz), nz), head)
        pl.semaphore_signal(barrier, inc=1, device_id=target, device_id_type=MESH)

    pl.semaphore_wait(barrier, slots - 1 + nz - 1)


def fused_kernel(
    nz,
    heads,
    local_heads,
    tiles_ref,
    lengths_ref,
    key_ref,
    value_ref,
    query_ref,
    cot_ref,
    att_ref,
    dq_ref,
    out_ref,
    win,
    q_scr,
    c_scr,
    zbuf,
    sbuf,
    s_scr,
    p_scr,
    dp_own,
    cot_t,
    low_scr,
    att_scr,
    dq_scr,
    terms,
    rbuf,
    acc,
    zsend,
    zrecv,
    res,
    load_sem,
    send_sem,
    recv_sem,
):
    quad, z, head, slot = place(nz, heads)
    slots, part, width2 = win.shape[1:]
    width = width2 // 2
    rows = query_ref.shape[0]
    tile_rows = slots * part
    scale = float(width) ** -0.5
    log_scale = scale * math.log2(math.e)

    def plane_target(step):
        other = lax.rem(slot + step, slots)
        other_quad = lax.div(other, heads)
        return other, other_quad, (ctx_of(other_quad, z, nz), lax.rem(other, heads))

    def arrived(phase, like):
        pltpu.make_async_copy(like, like, recv_sem.at[phase]).wait()
        pltpu.make_async_copy(like, like, send_sem.at[phase]).wait()

    loads = (
        pltpu.make_async_copy(key_ref, win.at[BACK, :, :, 0:width], load_sem.at[0]),
        pltpu.make_async_copy(value_ref, win.at[BACK, :, :, width:width2], load_sem.at[1]),
        pltpu.make_async_copy(query_ref, q_scr, load_sem.at[2]),
        pltpu.make_async_copy(cot_ref, c_scr, load_sem.at[3]),
    )
    for copy in loads:
        copy.start()
    greet(quad, z, head, slot, nz, heads)
    loads[0].wait()
    loads[1].wait()

    for step in range(1, 4):
        other = lax.rem(quad + step, 4)
        pltpu.make_async_remote_copy(
            src_ref=win.at[BACK, other * heads + head],
            dst_ref=zbuf.at[z, quad],
            send_sem=send_sem.at[0],
            recv_sem=recv_sem.at[0],
            device_id=(ctx_of(other, z, nz), head),
            device_id_type=MESH,
        ).start()
    mine = pltpu.make_async_copy(win.at[BACK, slot], zbuf.at[z, quad], load_sem.at[0])
    mine.start()
    mine.wait()
    arrived(0, zbuf.at[0, 0:3])

    @pl.loop(1, nz)
    def _(step):
        pltpu.make_async_remote_copy(
            src_ref=zbuf.at[z],
            dst_ref=zbuf.at[z],
            send_sem=send_sem.at[1],
            recv_sem=recv_sem.at[1],
            device_id=(ctx_of(quad, lax.rem(z + step, nz), nz), head),
            device_id_type=MESH,
        ).start()

    wanted = []
    for other in range(4):
        tile = tiles_ref[ctx_of(other, z, nz)]
        for back in range(BACK):
            wanted.append(jnp.maximum(tile - BACK + back, 0))

    def find(index, found):
        tile = tiles_ref[index]
        return tuple(jnp.where(tile == want, index, have) for want, have in zip(wanted, found))

    holders = lax.fori_loop(0, 4 * nz, find, tuple(jnp.int32(0) for _ in wanted))

    loads[2].wait()
    loads[3].wait()
    tile = tiles_ref[ctx_of(quad, z, nz)]
    base = (tile - BACK) * tile_rows
    high = lax.broadcasted_iota(jnp.int32, (1, rows), 1) // local_heads
    pos = tile * tile_rows + high
    low = jnp.zeros_like(pos)
    end = jnp.int32(0)
    for index in range(lengths_ref.shape[0]):
        end = end + lengths_ref[index]
        low = jnp.where(pos >= end, end, low)
    low_scr[...] = low - base
    at = lax.broadcasted_iota(jnp.int32, (tile_rows, rows), 0)

    def keys_of(block):
        return win[block, :, :, 0:width].reshape(tile_rows, width)

    def values_of(block):
        return win[block, :, :, width:width2].reshape(tile_rows, width)

    def scores(block, top):
        s = dot(keys_of(block), q_scr[...], ((1,), (1,)))
        live = at >= low_scr[...] - block * tile_rows
        if block == BACK:
            live = live & (at <= high)
        s = jnp.where(live, s, NEG_FILL)
        s_scr[block] = s
        return jnp.maximum(top, jnp.max(s.reshape(tile_rows // 8, 8, rows), axis=0))

    top = scores(BACK, jnp.full((8, rows), NEG_FILL, jnp.float32))
    cot_t[...] = c_scr[...].astype(jnp.float32).T
    dp_own[...] = dot(values_of(BACK), c_scr[...], ((1,), (1,)))

    arrived(1, zbuf.at[0 : nz - 1])

    for other in range(4):
        for back in range(BACK):
            holder = holders[other * BACK + back]
            from_z = lax.rem(lax.div(holder, 2), nz)
            from_quad = lax.div(holder, 2 * nz) * 2 + lax.rem(holder, 2)
            sbuf[other, back] = zbuf[from_z, from_quad]

    @pl.loop(1, slots)
    def _(step):
        other, other_quad, target = plane_target(step)
        pltpu.make_async_remote_copy(
            src_ref=sbuf.at[other_quad],
            dst_ref=win.at[0:BACK, slot],
            send_sem=send_sem.at[2],
            recv_sem=recv_sem.at[2],
            device_id=target,
            device_id_type=MESH,
        ).start()

    mine = pltpu.make_async_copy(sbuf.at[quad], win.at[0:BACK, slot], load_sem.at[0])
    mine.start()
    mine.wait()
    arrived(2, win.at[0:BACK, 0 : slots - 1])

    for block in range(BACK):
        top = scores(block, top)
    top = jnp.max(top, axis=0, keepdims=True) * log_scale
    total = jnp.zeros((8, rows), jnp.float32)
    out = jnp.zeros((width, rows), jnp.float32)
    for block in range(BACK + 1):
        p = jnp.exp2(s_scr[block] * log_scale - top)
        total = total + jnp.sum(p.reshape(tile_rows // 8, 8, rows), axis=0)
        p_low = p.astype(jnp.bfloat16)
        p_scr[block] = p_low
        out = out + dot(values_of(block), p_low, ((0,), (0,)))
    inverse = 1.0 / jnp.sum(total, axis=0, keepdims=True)
    out = (out * inverse).astype(jnp.bfloat16).astype(jnp.float32)
    att_scr[...] = out.T.astype(jnp.bfloat16)
    att_copy = pltpu.make_async_copy(att_scr, att_ref, load_sem.at[0])
    att_copy.start()
    cot = cot_t[...]
    delta = jnp.sum(cot * out, axis=0, keepdims=True) * inverse
    cot_scaled = cot * inverse
    cot_low = cot_scaled.astype(jnp.bfloat16)
    cot_rows = cot_scaled.T.astype(jnp.bfloat16)
    dq = jnp.zeros((width, rows), jnp.float32)
    for block in range(BACK + 1):
        p_low = p_scr[block]
        if block == BACK:
            dp = dp_own[...] * inverse
        else:
            dp = dot(values_of(block), cot_low, ((1,), (0,)))
        ds = (p_low.astype(jnp.float32) * (dp - delta)).astype(jnp.bfloat16)
        dv = dot(p_low, cot_rows, ((1,), (0,))).astype(jnp.bfloat16)
        dk = (dot(ds, q_scr[...], ((1,), (0,))) * scale).astype(jnp.bfloat16)
        terms[block, :, :, 0:width] = dk.reshape(slots, part, width)
        terms[block, :, :, width:width2] = dv.reshape(slots, part, width)
        dq = dq + dot(keys_of(block), ds, ((0,), (0,)))

    @pl.loop(1, slots)
    def _(step):
        other, other_quad, target = plane_target(step)
        pltpu.make_async_remote_copy(
            src_ref=terms.at[:, other],
            dst_ref=rbuf.at[slot],
            send_sem=send_sem.at[3],
            recv_sem=recv_sem.at[3],
            device_id=target,
            device_id_type=MESH,
        ).start()

    mine = pltpu.make_async_copy(terms.at[:, slot], rbuf.at[slot], load_sem.at[1])
    mine.start()
    dq_scr[...] = (dq * scale).T.astype(jnp.bfloat16)
    dq_copy = pltpu.make_async_copy(dq_scr, dq_ref, load_sem.at[2])
    dq_copy.start()
    mine.wait()
    arrived(3, rbuf.at[0 : slots - 1])

    for other in range(4):
        for back in range(BACK + 1):
            summed = rbuf[other * heads, back].astype(jnp.float32)
            for index in range(1, heads):
                summed = summed + rbuf[other * heads + index, back].astype(jnp.float32)
            acc[other, back] = summed

    sources = [tiles_ref[ctx_of(other, z, nz)] - BACK for other in range(4)]

    @pl.loop(0, nz)
    def _(step):
        to_z = lax.rem(z + step, nz)
        for to_quad in range(4):
            to_tile = tiles_ref[ctx_of(to_quad, to_z, nz)]
            summed = None
            for other in range(4):
                back = to_tile - sources[other]
                inside = jnp.logical_and(back >= 0, back <= BACK)
                loaded = acc[other, jnp.clip(back, 0, BACK)]
                term = jnp.where(inside, loaded, 0.0)
                summed = term if summed is None else summed + term
            zsend[to_z, to_quad] = summed.astype(zsend.dtype)

    @pl.loop(1, nz)
    def _(step):
        to_z = lax.rem(z + step, nz)
        pltpu.make_async_remote_copy(
            src_ref=zsend.at[to_z],
            dst_ref=zrecv.at[z],
            send_sem=send_sem.at[4],
            recv_sem=recv_sem.at[4],
            device_id=(ctx_of(quad, to_z, nz), head),
            device_id_type=MESH,
        ).start()

    mine = pltpu.make_async_copy(zsend.at[z], zrecv.at[z], load_sem.at[1])
    mine.start()
    mine.wait()
    arrived(4, zrecv.at[0 : nz - 1])
    summed = zrecv[0].astype(jnp.float32)
    for index in range(1, nz):
        summed = summed + zrecv[index].astype(jnp.float32)
    res[...] = summed.astype(res.dtype)

    @pl.loop(1, slots)
    def _(step):
        other, other_quad, target = plane_target(step)
        pltpu.make_async_remote_copy(
            src_ref=res.at[other_quad],
            dst_ref=out_ref.at[slot],
            send_sem=send_sem.at[5],
            recv_sem=recv_sem.at[5],
            device_id=target,
            device_id_type=MESH,
        ).start()

    mine = pltpu.make_async_copy(res.at[quad], out_ref.at[slot], load_sem.at[1])
    mine.start()
    mine.wait()
    att_copy.wait()
    dq_copy.wait()
    arrived(5, out_ref.at[0 : slots - 1])


def on_device(ctx_count, heads, queries, keys, values, grad_out, lengths, tile_of):
    tile_rows, local_heads, width = queries.shape
    rows = tile_rows * local_heads
    nz = ctx_count // 4
    slots = 4 * heads
    part = tile_rows // slots
    block = (part, 2 * width)
    low = keys.dtype
    smem = pl.BlockSpec(memory_space=pltpu.SMEM)
    anywhere = pl.BlockSpec(memory_space=pl.ANY)
    flat = jax.ShapeDtypeStruct((rows, width), low)
    attended, query_grad, sums = pl.pallas_call(
        functools.partial(fused_kernel, nz, heads, local_heads),
        out_shape=(flat, flat, jax.ShapeDtypeStruct((slots,) + block, low)),
        in_specs=[smem, smem, anywhere, anywhere, anywhere, anywhere],
        out_specs=(anywhere, anywhere, pl.BlockSpec(memory_space=pltpu.VMEM)),
        scratch_shapes=[
            pltpu.VMEM((BACK + 1, slots) + block, low),
            pltpu.VMEM((rows, width), low),
            pltpu.VMEM((rows, width), low),
            pltpu.VMEM((nz, 4) + block, low),
            pltpu.VMEM((4, BACK) + block, low),
            pltpu.VMEM((BACK + 1, tile_rows, rows), jnp.float32),
            pltpu.VMEM((BACK + 1, tile_rows, rows), low),
            pltpu.VMEM((tile_rows, rows), jnp.float32),
            pltpu.VMEM((width, rows), jnp.float32),
            pltpu.VMEM((1, rows), jnp.int32),
            pltpu.VMEM((rows, width), low),
            pltpu.VMEM((rows, width), low),
            pltpu.VMEM((BACK + 1, slots) + block, low),
            pltpu.VMEM((slots, BACK + 1) + block, low),
            pltpu.VMEM((4, BACK + 1) + block, jnp.float32),
            pltpu.VMEM((nz, 4) + block, low),
            pltpu.VMEM((nz, 4) + block, low),
            pltpu.VMEM((4,) + block, low),
            pltpu.SemaphoreType.DMA((4,)),
            pltpu.SemaphoreType.DMA((6,)),
            pltpu.SemaphoreType.DMA((6,)),
        ],
        compiler_params=pltpu.CompilerParams(
            collective_id=0, has_side_effects=True, vmem_limit_bytes=48 * 1024 * 1024
        ),
        name="ring_free_attention",
    )(
        tile_of,
        lengths,
        keys.reshape(slots, part, width),
        values.reshape(slots, part, width),
        queries.reshape(rows, width),
        grad_out.reshape(rows, width),
    )
    sums = sums.reshape(tile_rows, 2 * width)
    return (
        attended.reshape(queries.shape),
        query_grad.reshape(queries.shape),
        sums[:, :width].astype(jnp.float32),
        sums[:, width:].astype(jnp.float32),
    )


def solution(mesh):
    return jax.shard_map(
        functools.partial(on_device, mesh.shape["ctx"], mesh.shape["head"]),
        mesh=mesh,
        in_specs=(
            P("ctx", "head", None),
            P("ctx", None),
            P("ctx", None),
            P("ctx", "head", None),
            P(),
            P(),
        ),
        out_specs=(P("ctx", "head", None), P("ctx", "head", None), P("ctx", None), P("ctx", None)),
        check_vma=False,
    )
```

time: 593 us -> 84.8 us (0.14); the launches traced: 587 us -> 84.7 us
  waiting for transfers between devices: 231 us -> 0 us
  other arithmetic: 137 us -> 0.83 us
  matrix products: 97.5 us -> 0 us
  Pallas kernels: 0 us -> 77.4 us
  loops' own time: 56 us -> 0 us
  local copies, waits for them, and re-layouts: 50.7 us -> 5.77 us
  between operations: 14.5 us -> 0.66 us
    reduce_scatter x1 -> x0, waiting for transfers between devices: 152 us -> none  [on_device(): lax.psum_scatter(pieces.reshape(row_count, 2 * head_width), 'ctx', scatte...]
    reduce_or x64 -> x0, other arithmetic: 127 us -> none  [the longest x16 32.1 us: query_step(): alive = jnp.any(live_test(query_pos, query_doc, block_pos, block_doc))]
    dot_general x28 -> x0, matrix products: 97.5 us -> none  [the longest x12 36.2 us: contract_last(): lax.dot_general(left, right, (((1,), (1,)), ((), ())), preferred_element_...]
    pallas_call x0 -> x1, Pallas kernels: none -> 77.4 us  [on_device(): pl.pallas_call(functools.partial(fused_kernel, nz, heads, local_heads), o...]
    all_gather x2 -> x0, waiting for transfers between devices: 67.5 us -> none  [the longest x1 53.9 us: on_device(): lax.all_gather(keys, 'ctx', axis=0, tiled=True)]
    another operation x68 -> x0, loops' own time: 56 us -> none  [the longest x1 21.5 us: on_device(): lax.map(one_block, jnp.arange(row_count // sub_rows, dtype=jnp.int32))]
    dynamic_update_slice x32 -> x0, local copies, waits for them, and re-layouts: 22.4 us -> none  [on_device(): lax.map(one_block, jnp.arange(row_count // sub_rows, dtype=jnp.int32))]
    gather x2 -> x0, local copies, waits for them, and re-layouts: 13.7 us -> none  [the longest x1 6.86 us: on_device(): query_doc = jnp.repeat(tile_doc, local_heads, total_repeat_length=row_total)]
  transfers between devices with their start and end apart: 4 -> 0, of which waited for: 4 -> 0; matrix products, arithmetic and copies ran while one was open for 21% -> 0% of each run, Pallas kernels for 0% -> 0%
where the time goes in v3:
time: 84.8 us; the launch traced here: 84.7 us
  Pallas kernels  77.4 us (91%)
  local copies, waits for them, and re-layouts  5.77 us (7%)
    pallas_call x1, Pallas kernels, on_device(): pl.pallas_call(functools.partial(fused_kernel, nz, heads, local_heads), o...  77.4 us
    unnamed x14, local copies, waits for them, and re-layouts  5.77 us

profile of v3, /device:TPU:1, one launch (start us, length us, event | category | flops | bytes accessed | tf_op | source)
XLA Modules:
  0.0 84.7 jit_solution(14300954461099685906)
XLA Ops:
  0.6 0.0 copy-start.4
  0.6 0.0 copy-start.5
  0.7 0.6 copy-done.4
  1.3 0.0 copy-done.5
  1.3 0.0 copy-start
  1.3 0.9 %copy-done = bf16[512,2,128]{2,1,0:T(2,128)(2,1)S(1)} copy-done((bf16[512,2,128]{2,1,0:T(2,128)(2,1)S(1)}, bf16[512,2,128]{2,1,0:T(2,128)(2,1)}, u32[]{:S(2)}) %copy-start) | copy-done | bytes 262168
  2.3 0.0 copy-start.1
  2.3 0.9 %copy-done.1 = bf16[512,2,128]{2,1,0:T(2,128)(2,1)S(1)} copy-done((bf16[512,2,128]{2,1,0:T(2,128)(2,1)S(1)}, bf16[512,2,128]{2,1,0:T(2,128)(2,1)}, u32[]{:S(2)}) %copy-start.1) | copy-done | bytes 262168
  3.2 0.0 copy-start.2
  3.2 0.9 %copy-done.2 = bf16[512,128]{1,0:T(8,128)(2,1)S(1)} copy-done((bf16[512,128]{1,0:T(8,128)(2,1)S(1)}, bf16[512,128]{1,0:T(8,128)(2,1)}, u32[]{:S(2)}) %copy-start.2) | copy-done | bytes 131096
  4.1 0.0 copy-start.3
  4.1 0.9 %copy-done.3 = bf16[512,128]{1,0:T(8,128)(2,1)S(1)} copy-done((bf16[512,128]{1,0:T(8,128)(2,1)S(1)}, bf16[512,128]{1,0:T(8,128)(2,1)}, u32[]{:S(2)}) %copy-start.3) | copy-done | bytes 131096
  5.0 77.4 %ring_free_attention.1 = (bf16[1024,128]{1,0:T(8,128)(2,1)S(1)}, bf16[1024,128]{1,0:T(8,128)(2,1)S(1)}, bf16[32,16,256]{2,1,0:T(8,128)(2,1)S(1)}) custom-call(s32[32]{0:T(128)S(1)} %copy-done.4, s32[16]{0:T(128)S(1)} %copy-done.5, bf16[32,16,128]{2,1,0:T(8,128)(2,1)S(1)} %bitcast.12, bf16[32,16,128]{2,1,0:T(8,128)(2,1)S(1)} %bitcast.13, ...), custom_call_target="tpu_custom_call" | custom-call | tf_op jit(solution)/shard_map/ring_free_attention/pallas_call | solution.py:343
  82.4 0.8 slice_convert_fusion
  83.3 0.7 copy.12
  84.0 0.7 copy.13
Async XLA Ops:
  0.6 0.7 copy-start.4
  0.6 0.7 copy-start.5
  1.3 0.9 %copy-start = (bf16[512,2,128]{2,1,0:T(2,128)(2,1)S(1)}, bf16[512,2,128]{2,1,0:T(2,128)(2,1)}, u32[]{:S(2)}) copy-start(bf16[512,2,128]{2,1,0:T(2,128)(2,1)} %param.6) | copy-start | bytes 786436
  2.3 0.9 %copy-start.1 = (bf16[512,2,128]{2,1,0:T(2,128)(2,1)S(1)}, bf16[512,2,128]{2,1,0:T(2,128)(2,1)}, u32[]{:S(2)}) copy-start(bf16[512,2,128]{2,1,0:T(2,128)(2,1)} %param.9) | copy-start | bytes 786436
  3.2 0.9 %copy-start.2 = (bf16[512,128]{1,0:T(8,128)(2,1)S(1)}, bf16[512,128]{1,0:T(8,128)(2,1)}, u32[]{:S(2)}) copy-start(bf16[512,128]{1,0:T(8,128)(2,1)} %param.7) | copy-start | bytes 393220
  4.1 0.9 %copy-start.3 = (bf16[512,128]{1,0:T(8,128)(2,1)S(1)}, bf16[512,128]{1,0:T(8,128)(2,1)}, u32[]{:S(2)}) copy-start(bf16[512,128]{1,0:T(8,128)(2,1)} %param.8) | copy-start | bytes 393220
